TPU v7x, 512 devices: a whole 4x8x8 slice. The times are simulated.
512 devices in a mesh: rows: 64 (over y, x, core), cols: 8 (over z).
Axes of the slice: x: 4, y: 8, z: 8, core: 2. Of those that a mesh axis runs over, the one named last changes fastest.
Arguments:
- fact_cells: bfloat16 [3072, 32, 512], P('rows', 'cols'), may hold values from -6 to 6
- gain_col: float32 [512], replicated, may hold values from 0.1 to 1.9
- w_qkv: bfloat16 [512, 1536], replicated, may hold values from -0.25 to 0.25
- w_col_out: bfloat16 [512, 512], replicated, may hold values from -0.25 to 0.25
- gain_tile: float32 [512], replicated, may hold values from 0.1 to 1.9
- w_query: bfloat16 [512, 512], replicated, may hold values from -0.25 to 0.25
- w_tile_out: bfloat16 [512, 512], replicated, may hold values from -0.25 to 0.25
- tile_kv: bfloat16 [256, 128, 8, 128], P('rows', None, 'cols'), may hold values from -70 to 70
- tile_ids: int32 [64, 48], P('rows'), may hold values from -1 to 255, as said below
- key_mask: int32 [3072, 48], P('rows'), may hold values from 0 to 1, as said below
Outputs:
- layer_out: bfloat16 [3072, 32, 512], P('rows', 'cols')
Inputs may be any that keep to these rules, and one draw needn't show every extreme that they name: `tile_ids`: tile t is held by index t // 4 of rows. In every block the first slots, 36 of them or more, hold distinct tile ids and the rest hold -1; some block fills all 48 slots. The listed tiles of one block are held by distinct indices of rows. `key_mask`: 0 wherever the row's block holds -1 in that slot; 1 in slot 0 of every row.
All inputs are finite; a program needn't handle non-finite values.
Results may differ from a plain program's by a relative error of at most 0.023.
The roundings to bfloat16 on the way count: a program that leaves them out, or rounds other values in their place, can miss the bound.
Values may be sent and summed in bfloat16 or wider, within the bound.
A program may use at most 64 MiB of HBM per device.

v0:
```python
import jax
import jax.numpy as jnp
from jax import lax
from jax.sharding import PartitionSpec as P


def rms_scale(values, gain_vec):
    mean_sq = jnp.mean(values * values, axis=-1, keepdims=True)
    return values * lax.rsqrt(mean_sq + 1e-05) * gain_vec


def soft_weights(scores, axes):
    row_top = jnp.max(scores, axis=axes, keepdims=True)
    expo_vals = jnp.exp(scores - row_top)
    return (expo_vals / jnp.sum(expo_vals, axis=axes, keepdims=True)).astype(jnp.bfloat16)


def column_attend(queries, keyvals, head_size):
    key_part = keyvals[..., :head_size]
    val_part = keyvals[..., head_size:]
    scores = jnp.einsum(
        "rchd,rkhd->rhck", queries, key_part, preferred_element_type=jnp.float32
    ) * head_size ** (-0.5)
    col_weights = soft_weights(scores, (3,))
    return jnp.einsum(
        "rhck,rkhd->rchd", col_weights, val_part, preferred_element_type=jnp.float32
    ).astype(jnp.bfloat16)


def tile_attend(queries, fetched, key_mask, head_size):
    key_part = fetched[..., :head_size]
    val_part = fetched[..., head_size:]
    row_count, col_count, head_count = queries.shape[:3]
    q_blocks = queries.reshape(row_count // 4, 4, col_count, head_count, head_size)
    m_blocks = key_mask.reshape(row_count // 4, 4, key_mask.shape[1])

    def one_block(block_pair):
        block_q, block_m = block_pair
        scores = jnp.einsum(
            "rchd,tkhd->rchtk", block_q, key_part, preferred_element_type=jnp.float32
        ) * head_size ** (-0.5)
        live_keys = (block_m > 0)[:, None, None, :, None]
        scores = jnp.where(live_keys, scores, -1e30)
        tile_weights = soft_weights(scores, (3, 4))
        return jnp.einsum(
            "rchtk,tkhd->rchd", tile_weights, val_part, preferred_element_type=jnp.float32
        ).astype(jnp.bfloat16)

    answer = lax.map(one_block, (q_blocks, m_blocks))
    return answer.reshape(row_count, col_count, head_count, head_size)


def fetch_all(tile_kv, tile_ids):
    gathered = lax.all_gather(tile_kv, "rows", axis=0, tiled=True)
    return jnp.take(gathered, jnp.maximum(tile_ids[0], 0), axis=0)


def project(normed, weight):
    return jnp.dot(normed.reshape(-1, weight.shape[0]), weight, preferred_element_type=jnp.float32)


def shards(
    fact_cells,
    gain_col,
    w_qkv,
    w_col_out,
    gain_tile,
    w_query,
    w_tile_out,
    tile_kv,
    tile_ids,
    key_mask,
):
    model_width = fact_cells.shape[2]
    head_size = tile_kv.shape[3] // 2
    heads_all = model_width // head_size
    fetched = fetch_all(tile_kv, tile_ids)
    row_count, col_local = (fact_cells.shape[0], fact_cells.shape[1])
    residual = fact_cells.astype(jnp.float32)
    normed = rms_scale(residual, gain_col).astype(jnp.bfloat16)
    packed = (
        project(normed, w_qkv)
        .astype(jnp.bfloat16)
        .reshape(row_count, col_local, 3, heads_all, head_size)
    )
    queries = packed[:, :, 0]
    keyvals = jnp.concatenate([packed[:, :, 1], packed[:, :, 2]], axis=-1)
    queries_h, keyvals_h = (
        lax.all_to_all(queries, "cols", split_axis=2, concat_axis=1, tiled=True),
        lax.all_to_all(keyvals, "cols", split_axis=2, concat_axis=1, tiled=True),
    )
    mixed_col = column_attend(queries_h, keyvals_h, head_size)
    mixed_back = lax.all_to_all(mixed_col, "cols", split_axis=1, concat_axis=2, tiled=True)
    residual = residual + project(mixed_back, w_col_out).reshape(residual.shape)
    normed2 = rms_scale(residual, gain_tile).astype(jnp.bfloat16)
    asked_q = (
        project(normed2, w_query)
        .astype(jnp.bfloat16)
        .reshape(row_count, col_local, heads_all, head_size)
    )
    asked_h = lax.all_to_all(asked_q, "cols", split_axis=2, concat_axis=1, tiled=True)
    answer = tile_attend(asked_h, fetched, key_mask, head_size)
    answer_back = lax.all_to_all(answer, "cols", split_axis=1, concat_axis=2, tiled=True)
    final_out = residual + project(answer_back, w_tile_out).reshape(residual.shape)
    return final_out.astype(jnp.bfloat16)


def solution(mesh):
    placed = (
        P("rows", "cols", None),
        P(),
        P(),
        P(),
        P(),
        P(),
        P(),
        P("rows", None, "cols", None),
        P("rows", None),
        P("rows", None),
    )
    return jax.shard_map(
        shards, mesh=mesh, in_specs=placed, out_specs=P("rows", "cols", None), check_vma=False
    )
```

profile of v0, /device:TPU:8, one launch (start us, length us, event | category | flops | bytes accessed | tf_op | source)
XLA Modules:
  0.0 198.4 jit_solution(1383678545264350636)
XLA Ops:
  7.3 1.1 fusion.30
  8.3 1.1 fusion.32
  11.1 1.0 reshape.174
  12.1 10.3 %all-to-all-start.1 = ((bf16[8,2,6144]{2,1,0:T(2,128)(2,1)}), bf16[8,2,6144]{2,1,0:T(2,128)(2,1)S(1)}, u32[]{:S(2)}, u32[]{:S(2)}) async-start(bf16[8,2,6144]{2,1,0:T(2,128)(2,1)} %reshape.174), calls=%async_computation.1 | async-start | bytes 393216 | tf_op jit(solution)/shard_map/all_to_all | solution.py:89
  22.8 1.3 pad_maximum_fusion
  24.2 8.8 %all-to-all-done.1 = bf16[8,2,6144]{2,1,0:T(2,128)(2,1)S(1)} async-done(((bf16[8,2,6144]{2,1,0:T(2,128)(2,1)}), bf16[8,2,6144]{2,1,0:T(2,128)(2,1)S(1)}, u32[]{:S(2)}, u32[]{:S(2)}) %all-to-all-start.1) | async-done | bytes 196640 | tf_op jit(solution)/shard_map/all_to_all | solution.py:89
  32.9 3.5 %all-to-all-start = ((bf16[48,4,8,128]{3,1,0,2:T(4,128)(2,1)}), bf16[48,4,8,128]{3,1,0,2:T(4,128)(2,1)S(1)}, u32[]{:S(2)}, u32[]{:S(2)}) async-start(bf16[48,4,8,128]{3,1,0,2:T(4,128)(2,1)} %pad_maximum_fusion), calls=%async_computation | async-start | bytes 786432 | tf_op jit(solution)/shard_map/all_to_all | solution.py:90
  37.0 12.4 %all-to-all-done = bf16[48,4,8,128]{3,1,0,2:T(4,128)(2,1)S(1)} async-done(((bf16[48,4,8,128]{3,1,0,2:T(4,128)(2,1)}), bf16[48,4,8,128]{3,1,0,2:T(4,128)(2,1)S(1)}, u32[]{:S(2)}, u32[]{:S(2)}) %all-to-all-start) | async-done | bytes 393248 | tf_op jit(solution)/shard_map/all_to_all | solution.py:90
  49.5 1.3 fusion.38
  50.8 1.6 fusion.26
  52.9 12.2 %all_to_all.78 = bf16[8,2,6144]{2,1,0:T(2,128)(2,1)S(1)} all-to-all(bf16[8,2,6144]{2,1,0:T(2,128)(2,1)S(1)} %reshape.176), channel_id=1, replica_groups=mesh['rows'=64,'cols'=8] {'cols'}, dimensions={0} | all-to-all | bytes 393216 | tf_op jit(solution)/shard_map/all_to_all | solution.py:93
  66.7 1.3 convolution_convert_fusion.2
  68.4 1.0 reshape.178
  69.3 3.6 %all-to-all-start.3 = ((bf16[8,2,6144]{2,1,0:T(2,128)(2,1)}), bf16[8,2,6144]{2,1,0:T(2,128)(2,1)S(1)}, u32[]{:S(2)}, u32[]{:S(2)}) async-start(bf16[8,2,6144]{2,1,0:T(2,128)(2,1)} %reshape.178), calls=%async_computation.3 | async-start | bytes 393216 | tf_op jit(solution)/shard_map/all_to_all | solution.py:101
  73.0 9.4 %all-to-all-done.3 = bf16[8,2,6144]{2,1,0:T(2,128)(2,1)S(1)} async-done(((bf16[8,2,6144]{2,1,0:T(2,128)(2,1)}), bf16[8,2,6144]{2,1,0:T(2,128)(2,1)S(1)}, u32[]{:S(2)}, u32[]{:S(2)}) %all-to-all-start.3) | async-done | bytes 196640 | tf_op jit(solution)/shard_map/all_to_all | solution.py:101
  83.8 20.0 %all-gather.2.cloned.1.call-done = bf16[256,128,1,128]{3,1,2,0:T(8,128)(2,1)} async-done(((bf16[4,128,1,128]{3,1,2,0:T(8,128)(2,1)}), bf16[256,128,1,128]{3,1,2,0:T(8,128)(2,1)}) %all-gather.2.cloned.1.call-update) | async-done | bytes 8388624 | tf_op jit(solution)/shard_map/all_gather | solution.py:54
  103.8 4.2 %gather_fusion = bf16[48,128,128]{2,1,0:T(8,128)(2,1)S(1)} fusion(bf16[256,128,128]{2,1,0:T(8,128)(2,1)} %bitcast.194, s32[1024]{0:T(1024)S(1)} %pad_clamp_fusion), kind=kCustom, calls=%fused_computation | custom fusion | bytes 3145920 | tf_op jit(solution)/shard_map/jit(_take)/gather | solution.py:55
  108.3 1.9 fusion.36
  110.1 1.4 copy.66
  111.6 1.7 copy.65
  113.3 56.9 %while.10 = (s32[]{:T(128)}, bf16[12,4,32,1,64]{4,1,0,2,3:T(4,128)(2,1)}, s32[12,4,48]{2,1,0:T(4,128)}, bf16[12,4,32,1,64]{4,2,1,3,0:T(8,128)(2,1)}, bf16[48,128...) while((s32[]{:T(128)}, bf16[12,4,32,1,64]{4,1,0,2,3:T(4,128)(2,1)}, ...), condition=%wide.region_7.8_spmd, body=%wide.region_4.0_spmd.sunk | while | flops 210771904 | bytes 14258301 | solution.py:49
  114.0 1.5 fusion.56
  115.5 0.9 fusion.57
  116.5 1.0 fusion.58
  118.8 1.5 fusion.56
  121.2 1.0 fusion.58
  123.5 1.5 fusion.56
  125.9 1.0 fusion.58
  128.2 1.5 fusion.56
  130.7 1.0 fusion.58
  133.0 1.5 fusion.56
  135.4 1.0 fusion.58
  137.7 1.5 fusion.56
  140.1 1.0 fusion.58
  142.4 1.5 fusion.56
  144.9 1.0 fusion.58
  147.2 1.5 fusion.56
  149.6 1.0 fusion.58
  151.9 1.5 fusion.56
  154.4 1.0 fusion.58
  156.7 1.5 fusion.56
  159.1 1.0 fusion.58
  161.4 1.5 fusion.56
  163.9 1.0 fusion.58
  166.2 1.5 fusion.56
  168.6 1.0 fusion.58
  170.2 1.4 reshape.180
  171.6 18.1 %all_to_all.79 = bf16[8,2,6144]{2,1,0:T(2,128)(2,1)S(1)} all-to-all(bf16[8,2,6144]{2,1,0:T(2,128)(2,1)S(1)} %reshape.180), channel_id=1, replica_groups=mesh['rows'=64,'cols'=8] {'cols'}, dimensions={0} | all-to-all | bytes 393216 | tf_op jit(solution)/shard_map/all_to_all | solution.py:103
  (110 shorter events, 35.7 us)
Async XLA Ops:
  6.5 3.1 %copy-start = (bf16[512,1536]{1,0:T(8,128)(2,1)S(1)}, bf16[512,1536]{1,0:T(8,128)(2,1)}, u32[]{:S(2)}) copy-start(bf16[512,1536]{1,0:T(8,128)(2,1)} %param.14) | copy-start | bytes 4718596
  6.5 97.3 %all-gather.2.cloned.1.call-start = ((), (), s32[]{:S(2)}) async-start(), calls=%async_computation.5 | async-start | bytes 8519680 | tf_op jit(solution)/shard_map/all_gather | solution.py:54
  12.1 20.8 %all-to-all-start.1 = ((bf16[8,2,6144]{2,1,0:T(2,128)(2,1)}), bf16[8,2,6144]{2,1,0:T(2,128)(2,1)S(1)}, u32[]{:S(2)}, u32[]{:S(2)}) async-start(bf16[8,2,6144]{2,1,0:T(2,128)(2,1)} %reshape.174), calls=%async_computation.1 | async-start | bytes 393216 | tf_op jit(solution)/shard_map/all_to_all | solution.py:89
  32.9 16.4 %all-to-all-start = ((bf16[48,4,8,128]{3,1,0,2:T(4,128)(2,1)}), bf16[48,4,8,128]{3,1,0,2:T(4,128)(2,1)S(1)}, u32[]{:S(2)}, u32[]{:S(2)}) async-start(bf16[48,4,8,128]{3,1,0,2:T(4,128)(2,1)} %pad_maximum_fusion), calls=%async_computation | async-start | bytes 786432 | tf_op jit(solution)/shard_map/all_to_all | solution.py:90
  50.8 15.1 %copy-start.1 = (bf16[48,4,512]{2,1,0:T(4,128)(2,1)S(1)}, bf16[48,4,512]{2,1,0:T(4,128)(2,1)}, u32[]{:S(2)}) copy-start(bf16[48,4,512]{2,1,0:T(4,128)(2,1)} %param.12) | copy-start | bytes 589828
  50.8 15.1 %copy-start.3 = (bf16[512,512]{1,0:T(8,128)(2,1)S(1)}, bf16[512,512]{1,0:T(8,128)(2,1)}, u32[]{:S(2)}) copy-start(bf16[512,512]{1,0:T(8,128)(2,1)} %param.15) | copy-start | bytes 1572868
  52.4 13.9 %copy-start.5 = (f32[512]{0:T(512)S(1)}, f32[512]{0:T(512)}, u32[]{:S(2)}) copy-start(f32[512]{0:T(512)} %param.16) | copy-start | bytes 6148
  65.7 7.3 %copy-start.6 = (s32[1,48]{1,0:T(1,128)S(1)}, s32[1,48]{1,0:T(1,128)}, u32[]{:S(2)}) copy-start(s32[1,48]{1,0:T(1,128)} %param.20) | copy-start | bytes 580
  69.3 13.1 %all-to-all-start.3 = ((bf16[8,2,6144]{2,1,0:T(2,128)(2,1)}), bf16[8,2,6144]{2,1,0:T(2,128)(2,1)S(1)}, u32[]{:S(2)}, u32[]{:S(2)}) async-start(bf16[8,2,6144]{2,1,0:T(2,128)(2,1)} %reshape.178), calls=%async_computation.3 | async-start | bytes 393216 | tf_op jit(solution)/shard_map/all_to_all | solution.py:101
  114.0 2.4 %copy-start.2 = (bf16[48,128,1,64]{1,3,0,2:T(8,128)(2,1)S(1)}, bf16[48,128,1,64]{1,3,0,2:T(8,128)(2,1)}, u32[]{:S(2)}) copy-start(bf16[48,128,1,64]{1,3,0,2:T(8,128)(2,1)} %get-tuple-element.141) | copy-start | bytes 2359300 | tf_op jit(solution)/shard_map/while
  118.8 2.4 %copy-start.2 = (bf16[48,128,1,64]{1,3,0,2:T(8,128)(2,1)S(1)}, bf16[48,128,1,64]{1,3,0,2:T(8,128)(2,1)}, u32[]{:S(2)}) copy-start(bf16[48,128,1,64]{1,3,0,2:T(8,128)(2,1)} %get-tuple-element.141) | copy-start | bytes 2359300 | tf_op jit(solution)/shard_map/while
  123.5 2.4 %copy-start.2 = (bf16[48,128,1,64]{1,3,0,2:T(8,128)(2,1)S(1)}, bf16[48,128,1,64]{1,3,0,2:T(8,128)(2,1)}, u32[]{:S(2)}) copy-start(bf16[48,128,1,64]{1,3,0,2:T(8,128)(2,1)} %get-tuple-element.141) | copy-start | bytes 2359300 | tf_op jit(solution)/shard_map/while
  128.2 2.4 %copy-start.2 = (bf16[48,128,1,64]{1,3,0,2:T(8,128)(2,1)S(1)}, bf16[48,128,1,64]{1,3,0,2:T(8,128)(2,1)}, u32[]{:S(2)}) copy-start(bf16[48,128,1,64]{1,3,0,2:T(8,128)(2,1)} %get-tuple-element.141) | copy-start | bytes 2359300 | tf_op jit(solution)/shard_map/while
  133.0 2.4 %copy-start.2 = (bf16[48,128,1,64]{1,3,0,2:T(8,128)(2,1)S(1)}, bf16[48,128,1,64]{1,3,0,2:T(8,128)(2,1)}, u32[]{:S(2)}) copy-start(bf16[48,128,1,64]{1,3,0,2:T(8,128)(2,1)} %get-tuple-element.141) | copy-start | bytes 2359300 | tf_op jit(solution)/shard_map/while
  137.7 2.4 %copy-start.2 = (bf16[48,128,1,64]{1,3,0,2:T(8,128)(2,1)S(1)}, bf16[48,128,1,64]{1,3,0,2:T(8,128)(2,1)}, u32[]{:S(2)}) copy-start(bf16[48,128,1,64]{1,3,0,2:T(8,128)(2,1)} %get-tuple-element.141) | copy-start | bytes 2359300 | tf_op jit(solution)/shard_map/while
  142.4 2.4 %copy-start.2 = (bf16[48,128,1,64]{1,3,0,2:T(8,128)(2,1)S(1)}, bf16[48,128,1,64]{1,3,0,2:T(8,128)(2,1)}, u32[]{:S(2)}) copy-start(bf16[48,128,1,64]{1,3,0,2:T(8,128)(2,1)} %get-tuple-element.141) | copy-start | bytes 2359300 | tf_op jit(solution)/shard_map/while
  147.2 2.4 %copy-start.2 = (bf16[48,128,1,64]{1,3,0,2:T(8,128)(2,1)S(1)}, bf16[48,128,1,64]{1,3,0,2:T(8,128)(2,1)}, u32[]{:S(2)}) copy-start(bf16[48,128,1,64]{1,3,0,2:T(8,128)(2,1)} %get-tuple-element.141) | copy-start | bytes 2359300 | tf_op jit(solution)/shard_map/while
  151.9 2.4 %copy-start.2 = (bf16[48,128,1,64]{1,3,0,2:T(8,128)(2,1)S(1)}, bf16[48,128,1,64]{1,3,0,2:T(8,128)(2,1)}, u32[]{:S(2)}) copy-start(bf16[48,128,1,64]{1,3,0,2:T(8,128)(2,1)} %get-tuple-element.141) | copy-start | bytes 2359300 | tf_op jit(solution)/shard_map/while
  156.7 2.4 %copy-start.2 = (bf16[48,128,1,64]{1,3,0,2:T(8,128)(2,1)S(1)}, bf16[48,128,1,64]{1,3,0,2:T(8,128)(2,1)}, u32[]{:S(2)}) copy-start(bf16[48,128,1,64]{1,3,0,2:T(8,128)(2,1)} %get-tuple-element.141) | copy-start | bytes 2359300 | tf_op jit(solution)/shard_map/while
  161.4 2.4 %copy-start.2 = (bf16[48,128,1,64]{1,3,0,2:T(8,128)(2,1)S(1)}, bf16[48,128,1,64]{1,3,0,2:T(8,128)(2,1)}, u32[]{:S(2)}) copy-start(bf16[48,128,1,64]{1,3,0,2:T(8,128)(2,1)} %get-tuple-element.141) | copy-start | bytes 2359300 | tf_op jit(solution)/shard_map/while
  166.2 2.4 %copy-start.2 = (bf16[48,128,1,64]{1,3,0,2:T(8,128)(2,1)S(1)}, bf16[48,128,1,64]{1,3,0,2:T(8,128)(2,1)}, u32[]{:S(2)}) copy-start(bf16[48,128,1,64]{1,3,0,2:T(8,128)(2,1)} %get-tuple-element.141) | copy-start | bytes 2359300 | tf_op jit(solution)/shard_map/while
  170.2 20.3 %copy-start.4 = (bf16[512,512]{1,0:T(8,128)(2,1)S(1)}, bf16[512,512]{1,0:T(8,128)(2,1)}, u32[]{:S(2)}) copy-start(bf16[512,512]{1,0:T(8,128)(2,1)} %param.18) | copy-start | bytes 1572868
Sparse Core Ops, SparseCore 0:
  10.7 93.0 all-gather.1
where the time goes:
time: 200 us; the launch traced here: 198 us
  waiting for transfers between devices  51.3 us (26%)
  matrix products  34.6 us (17%)
  blocking collectives  30.2 us (15%)
  local copies, waits for them, and re-layouts  27.5 us (14%)
  other arithmetic  23.4 us (12%)
  starting transfers between devices  17.3 us (9%)
  between operations  13.8 us (7%)
    all_gather x1, waiting for transfers between devices, fetch_all(): gathered = lax.all_gather(tile_kv, 'rows', axis=0, tiled=True)  20 us
    all_to_all x1, blocking collectives, shards(): lax.all_to_all(answer, 'cols', split_axis=1, concat_axis=2, tiled=True)  18.1 us
    dot_general x12, matrix products, one_block(): jnp.einsum('rchd,tkhd->rchtk', block_q, key_part, preferred_element_type=...  17.6 us
    all_to_all x1, waiting for transfers between devices, shards(): lax.all_to_all(keyvals, 'cols', split_axis=2, concat_axis=1, tiled=True)  12.4 us
    all_to_all x1, blocking collectives, shards(): lax.all_to_all(mixed_col, 'cols', split_axis=1, concat_axis=2, tiled=True)  12.2 us
    dot_general x12, matrix products, one_block(): jnp.einsum('rchtk,tkhd->rchd', tile_weights, val_part, preferred_element_...  11.6 us
    reduce_sum x12, other arithmetic, soft_weights(): jnp.sum(expo_vals, axis=axes, keepdims=True)  11.4 us
    all_to_all x1, starting transfers between devices, shards(): lax.all_to_all(queries, 'cols', split_axis=2, concat_axis=1, tiled=True)  10.3 us
  transfers between devices with their start and end apart: 4, of which 4 were waited for; matrix products, arithmetic and copies ran while one was open for 8% of the time, Pallas kernels for 0%

commit v1 on v0

--- a/solution.py
+++ b/solution.py
@@ -51,7 +51,8 @@
 
 
 def fetch_all(tile_kv, tile_ids):
-    gathered = lax.all_gather(tile_kv, "rows", axis=0, tiled=True)
+    outgoing = jnp.stack([tile_kv] * lax.axis_size("rows"))
+    gathered = jnp.concatenate(lax.all_to_all(outgoing, "rows", 0, 0), axis=0)
     return jnp.take(gathered, jnp.maximum(tile_ids[0], 0), axis=0)
 
 

time: 200 us -> 362 us (1.81)
  the two profiles are of different devices: /device:TPU:8 before, /device:TPU:10 now
where the time goes in v1:
time: 362 us; the launch traced here: 361 us
  waiting for transfers between devices  206 us (57%)
  blocking collectives  37.6 us (10%)
  matrix products  34.5 us (10%)
  local copies, waits for them, and re-layouts  33.6 us (9%)
  starting transfers between devices  24.6 us (7%)
  other arithmetic  23.5 us (6%)
    all_to_all x1, waiting for transfers between devices, fetch_all(): gathered = jnp.concatenate(lax.all_to_all(outgoing, 'rows', 0, 0), axis=0)  185 us
    dot_general x12, matrix products, one_block(): jnp.einsum('rchd,tkhd->rchtk', block_q, key_part, preferred_element_type=...  17.6 us
    all_to_all x1, blocking collectives, shards(): lax.all_to_all(answer, 'cols', split_axis=1, concat_axis=2, tiled=True)  13.3 us
    all_to_all x1, waiting for transfers between devices, shards(): lax.all_to_all(keyvals, 'cols', split_axis=2, concat_axis=1, tiled=True)  12.4 us
    all_to_all x1, blocking collectives, shards(): lax.all_to_all(asked_q, 'cols', split_axis=2, concat_axis=1, tiled=True)  12.2 us
    all_to_all x1, blocking collectives, shards(): lax.all_to_all(mixed_col, 'cols', split_axis=1, concat_axis=2, tiled=True)  12.2 us
    dot_general x12, matrix products, one_block(): jnp.einsum('rchtk,tkhd->rchd', tile_weights, val_part, preferred_element_...  11.6 us
    reduce_sum x12, other arithmetic, soft_weights(): jnp.sum(expo_vals, axis=axes, keepdims=True)  11.4 us
  transfers between devices with their start and end apart: 3, of which 3 were waited for; matrix products, arithmetic and copies ran while one was open for 1% of the time, Pallas kernels for 0%

profile of v1, /device:TPU:10, one launch (start us, length us, event | category | flops | bytes accessed | tf_op | source)
XLA Modules:
  0.0 360.8 jit_solution(2429163687524007425)
XLA Ops:
  0.0 1.2 fusion.30
  1.2 1.1 fusion.32
  4.0 1.0 reshape.182
  5.0 10.3 %all-to-all-start.1 = ((bf16[8,2,6144]{2,1,0:T(2,128)(2,1)}), bf16[8,2,6144]{2,1,0:T(2,128)(2,1)S(1)}, u32[]{:S(2)}, u32[]{:S(2)}) async-start(bf16[8,2,6144]{2,1,0:T(2,128)(2,1)} %reshape.182), calls=%async_computation.1 | async-start | bytes 393216 | tf_op jit(solution)/shard_map/all_to_all | solution.py:90
  15.7 1.3 pad_maximum_fusion
  17.0 8.8 %all-to-all-done.1 = bf16[8,2,6144]{2,1,0:T(2,128)(2,1)S(1)} async-done(((bf16[8,2,6144]{2,1,0:T(2,128)(2,1)}), bf16[8,2,6144]{2,1,0:T(2,128)(2,1)S(1)}, u32[]{:S(2)}, u32[]{:S(2)}) %all-to-all-start.1) | async-done | bytes 196640 | tf_op jit(solution)/shard_map/all_to_all | solution.py:90
  25.8 3.5 all-to-all-start
  29.8 12.4 %all-to-all-done = bf16[48,4,8,128]{3,1,0,2:T(4,128)(2,1)S(1)} async-done(((bf16[48,4,8,128]{3,1,0,2:T(4,128)(2,1)}), bf16[48,4,8,128]{3,1,0,2:T(4,128)(2,1)S(1)}, u32[]{:S(2)}, u32[]{:S(2)}) %all-to-all-start) | async-done | bytes 393248 | tf_op jit(solution)/shard_map/all_to_all | solution.py:91
  42.4 1.3 fusion.38
  43.7 1.6 fusion.26
  45.8 12.2 %all_to_all.83 = bf16[8,2,6144]{2,1,0:T(2,128)(2,1)S(1)} all-to-all(bf16[8,2,6144]{2,1,0:T(2,128)(2,1)S(1)} %reshape.184), channel_id=1, replica_groups=mesh['rows'=64,'cols'=8] {'cols'}, dimensions={0} | all-to-all | bytes 393216 | tf_op jit(solution)/shard_map/all_to_all | solution.py:94
  59.5 1.3 convolution_convert_fusion.2
  61.5 12.2 %all_to_all.84 = bf16[8,2,6144]{2,1,0:T(2,128)(2,1)S(1)} all-to-all(bf16[8,2,6144]{2,1,0:T(2,128)(2,1)S(1)} %reshape.186), channel_id=1, replica_groups=mesh['rows'=64,'cols'=8] {'cols'}, dimensions={0} | all-to-all | bytes 393216 | tf_op jit(solution)/shard_map/all_to_all | solution.py:102
  73.7 5.3 %stack.2 = bf16[64,4,128,1,128]{4,2,1,3,0:T(8,128)(2,1)} broadcast(bf16[4,128,128]{2,1,0:T(8,128)(2,1)S(1)} %bitcast.194), dimensions={1,2,4} | broadcast | bytes 8519680 | tf_op jit(solution)/shard_map/stack | solution.py:54
  79.0 10.9 %all-to-all-start.4 = ((bf16[64,4,128,1,128]{4,2,1,3,0:T(8,128)(2,1)}), bf16[64,4,128,1,128]{4,2,1,3,0:T(8,128)(2,1)}, u32[]{:S(2)}, u32[]{:S(2)}) async-start(bf16[64,4,128,1,128]{4,2,1,3,0:T(8,128)(2,1)} %stack.2), calls=%async_computation.4 | async-start | bytes 16777216 | tf_op jit(solution)/shard_map/all_to_all | solution.py:55
  91.3 185.0 %all-to-all-done.4 = bf16[64,4,128,1,128]{4,2,1,3,0:T(8,128)(2,1)} async-done(((bf16[64,4,128,1,128]{4,2,1,3,0:T(8,128)(2,1)}), bf16[64,4,128,1,128]{4,2,1,3,0:T(8,128)(2,1)}, u32[]{:S(2)}, u32[]{:S(2)}) %all-to-all-start.4) | async-done | bytes 8388640 | tf_op jit(solution)/shard_map/all_to_all | solution.py:55
  276.3 4.2 %gather_fusion = bf16[48,128,128]{2,1,0:T(8,128)(2,1)S(1)} fusion(bf16[256,128,128]{2,1,0:T(8,128)(2,1)} %bitcast.41, s32[1024]{0:T(1024)S(1)} %pad_clamp_fusion), kind=kCustom, calls=%fused_computation | custom fusion | bytes 3145920 | tf_op jit(solution)/shard_map/jit(_take)/gather | solution.py:56
  280.8 2.3 fusion.36
  283.1 1.7 copy.64
  284.9 2.5 copy.65
  287.3 56.9 %while.10 = (s32[]{:T(128)}, bf16[12,4,32,1,64]{4,1,0,2,3:T(4,128)(2,1)}, s32[12,4,48]{2,1,0:T(4,128)}, bf16[12,4,32,1,64]{4,2,1,3,0:T(8,128)(2,1)}, bf16[48,128...) while((s32[]{:T(128)}, bf16[12,4,32,1,64]{4,1,0,2,3:T(4,128)(2,1)}, ...), condition=%wide.region_7.8_spmd, body=%wide.region_4.0_spmd.sunk | while | flops 210771904 | bytes 14259309 | solution.py:49
  288.0 1.5 fusion.56
  290.5 1.0 fusion.58
  292.8 1.5 fusion.56
  295.2 1.0 fusion.58
  297.5 1.5 fusion.56
  299.9 1.0 fusion.58
  302.2 1.5 fusion.56
  304.7 1.0 fusion.58
  307.0 1.5 fusion.56
  308.5 0.9 fusion.57
  309.4 1.0 fusion.58
  311.7 1.5 fusion.56
  314.2 1.0 fusion.58
  316.5 1.5 fusion.56
  318.9 1.0 fusion.58
  321.2 1.5 fusion.56
  323.7 1.0 fusion.58
  326.0 1.5 fusion.56
  328.4 1.0 fusion.58
  330.7 1.5 fusion.56
  333.1 1.0 fusion.58
  335.5 1.5 fusion.56
  337.9 1.0 fusion.58
  340.2 1.5 fusion.56
  342.6 1.0 fusion.58
  344.2 1.4 reshape.188
  345.6 13.3 %all_to_all.85 = bf16[8,2,6144]{2,1,0:T(2,128)(2,1)S(1)} all-to-all(bf16[8,2,6144]{2,1,0:T(2,128)(2,1)S(1)} %reshape.188), channel_id=1, replica_groups=mesh['rows'=64,'cols'=8] {'cols'}, dimensions={0} | all-to-all | bytes 393216 | tf_op jit(solution)/shard_map/all_to_all | solution.py:104
  (111 shorter events, 35.3 us)
Async XLA Ops:
  0.0 2.5 copy-start
  5.0 20.8 %all-to-all-start.1 = ((bf16[8,2,6144]{2,1,0:T(2,128)(2,1)}), bf16[8,2,6144]{2,1,0:T(2,128)(2,1)S(1)}, u32[]{:S(2)}, u32[]{:S(2)}) async-start(bf16[8,2,6144]{2,1,0:T(2,128)(2,1)} %reshape.182), calls=%async_computation.1 | async-start | bytes 393216 | tf_op jit(solution)/shard_map/all_to_all | solution.py:90
  25.8 16.4 %all-to-all-start = ((bf16[48,4,8,128]{3,1,0,2:T(4,128)(2,1)}), bf16[48,4,8,128]{3,1,0,2:T(4,128)(2,1)S(1)}, u32[]{:S(2)}, u32[]{:S(2)}) async-start(bf16[48,4,8,128]{3,1,0,2:T(4,128)(2,1)} %pad_maximum_fusion), calls=%async_computation | async-start | bytes 786432 | tf_op jit(solution)/shard_map/all_to_all | solution.py:91
  43.7 15.1 %copy-start.1 = (bf16[48,4,512]{2,1,0:T(4,128)(2,1)S(1)}, bf16[48,4,512]{2,1,0:T(4,128)(2,1)}, u32[]{:S(2)}) copy-start(bf16[48,4,512]{2,1,0:T(4,128)(2,1)} %param.12) | copy-start | bytes 589828
  43.7 15.1 %copy-start.3 = (bf16[512,512]{1,0:T(8,128)(2,1)S(1)}, bf16[512,512]{1,0:T(8,128)(2,1)}, u32[]{:S(2)}) copy-start(bf16[512,512]{1,0:T(8,128)(2,1)} %param.15) | copy-start | bytes 1572868
  45.3 13.9 %copy-start.6 = (f32[512]{0:T(512)S(1)}, f32[512]{0:T(512)}, u32[]{:S(2)}) copy-start(f32[512]{0:T(512)} %param.16) | copy-start | bytes 6148
  58.8 14.9 %copy-start.5 = (bf16[4,128,1,128]{3,1,2,0:T(8,128)(2,1)S(1)}, bf16[4,128,1,128]{3,1,2,0:T(8,128)(2,1)}, u32[]{:S(2)}) copy-start(bf16[4,128,1,128]{3,1,2,0:T(8,128)(2,1)} %param.19) | copy-start | bytes 393220
  79.0 10.9 %copy-start.7 = (s32[1,48]{1,0:T(1,128)S(1)}, s32[1,48]{1,0:T(1,128)}, u32[]{:S(2)}) copy-start(s32[1,48]{1,0:T(1,128)} %param.20) | copy-start | bytes 580
  79.0 197.3 %all-to-all-start.4 = ((bf16[64,4,128,1,128]{4,2,1,3,0:T(8,128)(2,1)}), bf16[64,4,128,1,128]{4,2,1,3,0:T(8,128)(2,1)}, u32[]{:S(2)}, u32[]{:S(2)}) async-start(bf16[64,4,128,1,128]{4,2,1,3,0:T(8,128)(2,1)} %stack.2), calls=%async_computation.4 | async-start | bytes 16777216 | tf_op jit(solution)/shard_map/all_to_all | solution.py:55
  288.0 2.4 copy-start.2
  292.8 2.4 copy-start.2
  297.5 2.4 copy-start.2
  302.2 2.4 copy-start.2
  307.0 2.4 copy-start.2
  311.7 2.4 copy-start.2
  316.5 2.4 copy-start.2
  321.2 2.4 copy-start.2
  326.0 2.4 copy-start.2
  330.7 2.4 copy-start.2
  335.5 2.4 copy-start.2
  340.2 2.4 copy-start.2
  344.2 15.5 %copy-start.4 = (bf16[512,512]{1,0:T(8,128)(2,1)S(1)}, bf16[512,512]{1,0:T(8,128)(2,1)}, u32[]{:S(2)}) copy-start(bf16[512,512]{1,0:T(8,128)(2,1)} %param.18) | copy-start | bytes 1572868
